TPU v7x, 32 devices: a whole 2x2x4 slice. The times are simulated.
32 devices in a mesh: grp: 2 (over x), ctx: 16 (over z, y, core).
Axes of the slice: x: 2, y: 2, z: 4, core: 2. Of those that a mesh axis runs over, the one named last changes fastest.
Arguments:
- cache_keys: bfloat16 [2048, 512], P(('grp', 'ctx')), parts along dimension 0, may hold values from -4 to 4
- cache_values: bfloat16 [2048, 512], P(('grp', 'ctx')), parts along dimension 0, may hold values from -4 to 4
- new_queries: bfloat16 [2048, 4096], P(('grp', 'ctx')), parts along dimension 0, may hold values from -600 to 600
- new_keys: bfloat16 [2048, 512], P(('grp', 'ctx')), parts along dimension 0, may hold values from -4 to 4
- new_values: bfloat16 [2048, 512], P(('grp', 'ctx')), parts along dimension 0, may hold values from -4 to 4
- cont_queries: bfloat16 [64, 4096], P(('grp', 'ctx')), parts along dimension 0, may hold values from -600 to 600
- suffix_keys: bfloat16 [64, 128, 512], P(('grp', 'ctx')), parts along dimension 0, may hold values from -4 to 4
- suffix_values: bfloat16 [64, 128, 512], P(('grp', 'ctx')), parts along dimension 0, may hold values from -4 to 4
- window_start: int32 [2], P('grp'), parts along dimension 0, may hold values from 0 to 255
- prefix_length: int32 [2], P('grp'), parts along dimension 0, may hold values from 512 to 1024
- suffix_length: int32 [64], P(('grp', 'ctx')), parts along dimension 0, may hold values from 2 to 128
Outputs:
- prompt_out: bfloat16 [2048, 4096], P(('grp', 'ctx')), parts along dimension 0
- cont_out: bfloat16 [64, 4096], P(('grp', 'ctx')), parts along dimension 0
There are 2 independent parts, one for each index of `grp`. A program takes and returns all parts, laid end to end along the dimension named above; each array names one. Nothing has to cross between parts.
All inputs are finite; a program needn't handle non-finite values.
Results may differ from a plain program's by a relative error of at most 0.009.
Values may be sent and summed in bfloat16 or wider, within the bound.
No kernel may reach another device: no remote copies, remote signals or barrier semaphores. Data moves between devices by JAX's collectives and lax.ppermute only.
A program may use at most 192 MiB of HBM per device.

v0:
```python
import jax
import jax.numpy as jnp
from jax import lax
from jax.sharding import PartitionSpec as P

KVH = 4
HD = 128
GROUP = 8


def empty_running(row_count):
    return (
        jnp.full((row_count, KVH, GROUP), -1e30, jnp.float32),
        jnp.zeros((row_count, KVH, GROUP), jnp.float32),
        jnp.zeros((row_count, KVH, GROUP, HD), jnp.float32),
    )


def key_places(begin_row, row_count, cache_rows, prompt_rows, window_first, prefix_last):
    position = begin_row + jnp.arange(row_count, dtype=jnp.int32)
    stride = cache_rows + prompt_rows
    shard_index = position // stride
    within = position % stride
    in_cache = within < cache_rows
    cache_index = shard_index * cache_rows + within
    prompt_index = shard_index * prompt_rows + within - cache_rows
    cache_ok = in_cache & (cache_index >= window_first) & (cache_index < prefix_last)
    return (in_cache, cache_ok, prompt_index)


def attend_piece(running, queries, visible, key_piece, value_piece):
    row_max, row_sum, numerator = running
    count = key_piece.shape[0]
    key_heads = key_piece.reshape(count, KVH, HD)
    value_heads = value_piece.reshape(count, KVH, HD)
    scores = jnp.einsum(
        "rkgd,lkd->rkgl", queries, key_heads, preferred_element_type=jnp.float32
    ) * HD ** (-0.5)
    mask = visible[:, None, None, :]
    scores = jnp.where(mask, scores, -1e30)
    new_max = jnp.maximum(row_max, jnp.max(scores, axis=-1))
    probs = jnp.where(mask, jnp.exp(scores - new_max[..., None]), 0.0)
    row_sum = jnp.sum(probs, axis=-1)
    numerator = jnp.einsum(
        "rkgl,lkd->rkgd",
        probs.astype(jnp.bfloat16),
        value_heads,
        preferred_element_type=jnp.float32,
    )
    return (new_max, row_sum, numerator)


def combine_states(stacked, suffix_state):
    stack_max, stack_sum, stack_numer = stacked
    suffix_max, suffix_sum, suffix_numer = suffix_state
    highest = jnp.maximum(jnp.max(stack_max, axis=0), suffix_max)
    stack_weight = jnp.exp(stack_max - highest)
    suffix_weight = jnp.exp(suffix_max - highest)
    numerator = (
        jnp.sum(stack_numer * stack_weight[..., None], axis=0)
        + suffix_numer * suffix_weight[..., None]
    )
    denominator = jnp.sum(stack_sum * stack_weight, axis=0) + suffix_sum * suffix_weight
    return numerator / denominator[..., None]


def body(
    cache_keys,
    cache_values,
    new_queries,
    new_keys,
    new_values,
    cont_queries,
    suffix_keys,
    suffix_values,
    window_start,
    prefix_length,
    suffix_length,
):
    cache_rows = cache_keys.shape[0]
    prompt_rows = new_keys.shape[0]
    window_first = window_start[0]
    prefix_last = prefix_length[0]
    device_place = lax.axis_index("ctx")
    query_index = device_place * prompt_rows + jnp.arange(prompt_rows, dtype=jnp.int32)
    prompt_heads = new_queries.reshape(prompt_rows, KVH, GROUP, HD)
    local_keys = jnp.concatenate([cache_keys, new_keys], axis=0)
    local_values = jnp.concatenate([cache_values, new_values], axis=0)
    cont_count = cont_queries.shape[0]
    cont_heads = cont_queries.reshape(cont_count, KVH, GROUP, HD)
    suffix_rows = suffix_keys.shape[1]
    own_keys = suffix_keys.reshape(cont_count, suffix_rows, KVH, HD)
    own_values = suffix_values.reshape(cont_count, suffix_rows, KVH, HD)
    suffix_scores = jnp.einsum(
        "ckgd,cskd->ckgs", cont_heads, own_keys, preferred_element_type=jnp.float32
    ) * HD ** (-0.5)
    suffix_mask = (jnp.arange(suffix_rows, dtype=jnp.int32)[None, :] < suffix_length[:, None])[
        :, None, None, :
    ]
    suffix_scores = jnp.where(suffix_mask, suffix_scores, -1e30)
    suffix_max = jnp.max(suffix_scores, axis=-1)
    suffix_probs = jnp.where(suffix_mask, jnp.exp(suffix_scores - suffix_max[..., None]), 0.0)
    suffix_sum = jnp.sum(suffix_probs, axis=-1)
    suffix_numer = jnp.einsum(
        "ckgs,cskd->ckgd",
        suffix_probs.astype(jnp.bfloat16),
        own_values,
        preferred_element_type=jnp.float32,
    )
    suffix_state = (suffix_max, suffix_sum, suffix_numer)
    key_piece = lax.all_gather(local_keys, "ctx", axis=0, tiled=True)
    in_cache, cache_ok, prompt_index = key_places(
        jnp.int32(0), key_piece.shape[0], cache_rows, prompt_rows, window_first, prefix_last
    )
    visible = cache_ok[None, :] | (~in_cache)[None, :] & (
        prompt_index[None, :] <= query_index[:, None]
    )
    prompt_state = attend_piece(
        empty_running(prompt_rows),
        prompt_heads,
        visible,
        key_piece,
        lax.all_gather(local_values, "ctx", axis=0, tiled=True),
    )
    every_query = lax.all_gather(cont_queries, "ctx", axis=0, tiled=True)
    every_count = every_query.shape[0]
    every_heads = every_query.reshape(every_count, KVH, GROUP, HD)
    in_cache, cache_ok, prompt_index = key_places(
        device_place * (cache_rows + prompt_rows),
        local_keys.shape[0],
        cache_rows,
        prompt_rows,
        window_first,
        prefix_last,
    )
    visible = (cache_ok | ~in_cache)[None, :]
    local_max, local_sum, local_numer = attend_piece(
        empty_running(every_count), every_heads, visible, local_keys, local_values
    )
    exchanged = (
        lax.all_to_all(local_numer[None], "ctx", split_axis=1, concat_axis=0, tiled=True),
        lax.all_to_all(local_max[None], "ctx", split_axis=1, concat_axis=0, tiled=True),
        lax.all_to_all(local_sum[None], "ctx", split_axis=1, concat_axis=0, tiled=True),
    )
    stacked = (exchanged[1], exchanged[2], exchanged[0])
    prompt_max, prompt_sum, prompt_numer = prompt_state
    prompt_out = (
        (prompt_numer / prompt_sum[..., None])
        .reshape(prompt_rows, new_queries.shape[1])
        .astype(jnp.bfloat16)
    )
    cont_out = (
        combine_states(stacked, suffix_state)
        .reshape(cont_count, cont_queries.shape[1])
        .astype(jnp.bfloat16)
    )
    return (prompt_out, cont_out)


def solution(mesh):
    in_specs = (
        P(("grp", "ctx"), None),
        P(("grp", "ctx"), None),
        P(("grp", "ctx"), None),
        P(("grp", "ctx"), None),
        P(("grp", "ctx"), None),
        P(("grp", "ctx"), None),
        P(("grp", "ctx"), None, None),
        P(("grp", "ctx"), None, None),
        P("grp"),
        P("grp"),
        P(("grp", "ctx")),
    )
    out_specs = (P(("grp", "ctx"), None), P(("grp", "ctx"), None))
    return jax.shard_map(body, mesh=mesh, in_specs=in_specs, out_specs=out_specs, check_vma=False)
```

profile of v0, /device:TPU:0, one launch (start us, length us, event | category | flops | bytes accessed | tf_op | source)
XLA Modules:
  0.0 118.5 jit_solution(2128454379710857456)
XLA Ops:
  7.2 0.0 copy-start
  7.2 0.0 all-gather.6.cloned.1.call-start
  7.2 1.0 copy.85
  8.2 1.0 copy.86
  9.2 0.8 pad_maximum_fusion.1
  10.0 0.0 all-gather.6.cloned.1.call-update
  11.3 24.1 %all-gather = bf16[16,2,4096]{2,1,0:T(2,128)(2,1)S(1)} all-gather(bf16[1,2,4096]{2,1,0:T(2,128)(2,1)} %bitcast.110), channel_id=1, replica_groups=mesh['grp'=2,'ctx'=16] {'ctx'}, dimensions={0}, use_global_device_ids=true | all-gather | bytes 278528 | tf_op jit(solution)/shard_map/all_gather | solution.py:125
  35.4 0.2 reshape.240
  35.7 1.3 %fusion.56 = (f32[32,4,8]{0,2,1:T(8,128)S(1)}, f32[32,4,8,128]{3,0,2,1:T(8,128)S(1)}) fusion(bf16[128,4,128,1]{0,2,3,1:T(8,128)(2,1)} %bitcast.103, bf16[32,4,8,128]{3,2,1,0:T(8,128)(2,1)S(1)} %reshape.240, pred[128]{0:T(512)(128)(4,1)S(1)} %not_or_fusion), kind=kOutput, calls=%fused_computation.85 | convolution fusion | flops 33946624 | bytes 921728 | tf_op jit(solution)/shard_map/rkgd,lkd->rkgl/dot_general | solution.py:36
  37.0 0.4 fusion.21
  37.3 0.7 copy.104
  38.1 3.5 %all-to-all-start.2 = ((f32[1,32,4,8]{3,2,0,1:T(4,128)}), f32[1,32,4,8]{3,2,0,1:T(4,128)S(1)}, u32[]{:S(2)}, u32[]{:S(2)}) async-start(f32[1,32,4,8]{3,2,0,1:T(4,128)} %copy.104), calls=%async_computation.2 | async-start | bytes 131072 | tf_op jit(solution)/shard_map/all_to_all | solution.py:143
  41.6 0.0 all-gather.4.cloned.1.call-start
  41.6 1.0 copy.83
  42.6 1.0 copy.84
  43.5 0.8 pad_maximum_fusion
  44.3 0.0 all-gather.4.cloned.1.call-update
  44.3 0.7 iota_compare_fusion
  45.1 1.2 %convolution_bitcast_fusion = f32[1,32,4,8,128]{4,1,3,2,0:T(8,128)S(1)} fusion(bf16[128,4,128,1]{0,2,3,1:T(8,128)(2,1)} %bitcast.104, f32[32,4,8,128]{3,0,2,1:T(8,128)S(1)} %get-tuple-element.11, f32[32,4,8]{0,2,1:T(8,128)S(1)} %get-tuple-element.7, pred[128]{0:T(512)(128)(4,1)S(1)} %not_or_fusion), kind=kOutput, calls=%fused_computation.8 | convolution fusion | flops 33947648 | bytes 1183872 | tf_op jit(solution)/shard_map/rkgl,lkd->rkgd/dot_general | solution.py:44
  46.3 0.0 copy-done
  46.3 1.1 fusion.57
  47.4 0.2 fusion.32
  47.6 0.7 copy.95
  48.3 1.3 %all-to-all-done.2 = f32[1,32,4,8]{3,2,0,1:T(4,128)S(1)} async-done(((f32[1,32,4,8]{3,2,0,1:T(4,128)}), f32[1,32,4,8]{3,2,0,1:T(4,128)S(1)}, u32[]{:S(2)}, u32[]{:S(2)}) %all-to-all-start.2) | async-done | bytes 4128 | tf_op jit(solution)/shard_map/all_to_all | solution.py:143
  49.5 4.7 %all-to-all-start.1 = ((f32[1,32,4,8]{3,2,0,1:T(4,128)}), f32[1,32,4,8]{3,2,0,1:T(4,128)S(1)}, u32[]{:S(2)}, u32[]{:S(2)}) async-start(f32[1,32,4,8]{3,2,0,1:T(4,128)} %copy.95), calls=%async_computation.1 | async-start | bytes 131072 | tf_op jit(solution)/shard_map/all_to_all | solution.py:142
  54.2 1.1 copy.94
  55.3 1.1 copy.121
  56.5 4.6 %all-to-all-done.1 = f32[1,32,4,8]{3,2,0,1:T(4,128)S(1)} async-done(((f32[1,32,4,8]{3,2,0,1:T(4,128)}), f32[1,32,4,8]{3,2,0,1:T(4,128)S(1)}, u32[]{:S(2)}, u32[]{:S(2)}) %all-to-all-start.1) | async-done | bytes 4128 | tf_op jit(solution)/shard_map/all_to_all | solution.py:142
  61.1 3.6 %all-to-all-start = ((f32[1,32,4,8,128]{4,3,2,0,1:T(8,128)}), f32[1,32,4,8,128]{4,3,2,0,1:T(8,128)S(1)}, u32[]{:S(2)}, u32[]{:S(2)}) async-start(f32[1,32,4,8,128]{4,3,2,0,1:T(8,128)} %copy.94), calls=%async_computation | async-start | bytes 1048576 | tf_op jit(solution)/shard_map/all_to_all | solution.py:141
  64.7 0.2 and_or_fusion
  65.0 0.1 multiply_reduce_fusion
  65.1 0.5 copy.100
  65.5 16.9 %all-to-all-done = f32[1,32,4,8,128]{4,3,2,0,1:T(8,128)S(1)} async-done(((f32[1,32,4,8,128]{4,3,2,0,1:T(8,128)}), f32[1,32,4,8,128]{4,3,2,0,1:T(8,128)S(1)}, u32[]{:S(2)}, u32[]{:S(2)}) %all-to-all-start) | async-done | bytes 524320 | tf_op jit(solution)/shard_map/all_to_all | solution.py:141
  82.4 0.7 fusion.18
  83.1 1.2 %fusion.15 = bf16[1,2,32,128]{3,2,1,0:T(8,128)(2,1)S(1)} fusion(f32[2,4,8,128]{3,0,2,1:T(2,128)S(1)} %fusion.18, f32[2,4,8,128]{3,2,1,0:T(8,128)S(1)} %get-tuple-element.13, f32[2,4,8]{2,1,0:T(4,128)S(1)} %get-tuple-element.2, f32[2,4,8]{2,1,0:T(4,128)S(1)} %get-tuple-element.3, f32[2,4,8]{2,1,0:T(4,128)S(1)} %get-tuple-element.12, ...), kind=kOutput, calls=%fused_computation.18 | convolution fusion | flops 2154496 | bytes 345088 | tf_op jit(solution)/shard_map/ckgs,cskd->ckgd/dot_general | solution.py:104
  84.3 0.6 copy.161
  85.0 0.0 all-gather.6.cloned.1.call-done
  85.0 4.6 %fusion = (f32[64,4,8]{0,2,1:T(8,128)S(1)}, f32[4,2048,64,8]{1,2,3,0:T(8,128)S(1)}) fusion(pred[64,2048]{1,0:T(8,128)(4,1)S(1)} %and_or_fusion, bf16[2048,4,128,1]{0,2,3,1:T(8,128)(2,1)} %bitcast.102, bf16[64,4,8,128]{3,2,1,0:T(8,128)(2,1)S(1)} %bitcast.99), kind=kOutput, calls=%fused_computation.2 | convolution fusion | flops 1086322688 | bytes 19537920 | tf_op jit(solution)/shard_map/rkgd,lkd->rkgl/dot_general | solution.py:36
  89.6 0.0 copy-start.1
  89.6 5.7 %copy-done.1 = f32[4,2048,64,8]{1,2,3,0:T(8,128)} copy-done((f32[4,2048,64,8]{1,2,3,0:T(8,128)}, f32[4,2048,64,8]{1,2,3,0:T(8,128)S(1)}, u32[]{:S(2)}) %copy-start.1) | copy-done | bytes 16777240
  95.3 5.1 %fusion.1 = f32[64,4,8]{0,2,1:T(8,128)S(1)} fusion(f32[4,2048,64,8]{1,2,3,0:T(8,128)S(1)} %get-tuple-element.9, f32[64,4,8]{0,2,1:T(8,128)S(1)} %broadcast_maximum_fusion.1, pred[64,2048]{1,0:T(8,128)(4,1)S(1)} %and_or_fusion), kind=kLoop, calls=%fused_computation.3 | loop fusion | flops 20969472 | bytes 16924672 | tf_op jit(solution)/shard_map/reduce_sum | solution.py:43
  100.4 1.6 %all-gather.4.cloned.1.call-done = bf16[2048,512]{0,1:T(8,128)(2,1)} async-done(((bf16[128,512]{0,1:T(8,128)(2,1)}), bf16[2048,512]{0,1:T(8,128)(2,1)}) %all-gather.4.cloned.1.call-update) | async-done | bytes 2097168 | tf_op jit(solution)/shard_map/all_gather | solution.py:123
  102.0 8.3 %divide_convert_fusion = bf16[64,4,8,128]{3,0,2,1:T(8,128)(2,1)S(1)} fusion(bf16[2048,4,128,1]{0,2,3,1:T(8,128)(2,1)} %bitcast.114, f32[4,2048,64,8]{1,2,3,0:T(8,128)} %copy-done.1, f32[64,4,8]{0,2,1:T(8,128)S(1)} %broadcast_maximum_fusion.1, pred[64,2048]{1,0:T(8,128)(4,1)S(1)} %and_or_fusion, f32[64,4,8]{0,2,1:T(8,128)S(1)} %fusion.1), kind=kOutput, calls=%fused_computation.19 | convolution fusion | flops 1095237632 | bytes 19546112 | tf_op jit(solution)/shard_map/rkgl,lkd->rkgd/dot_general | solution.py:44
  110.3 0.3 copy.90
  110.7 1.0 copy.160
  (12 shorter events, 0.1 us)
Async XLA Ops:
  7.2 39.1 %copy-start = (bf16[2,128,512]{2,1,0:T(8,128)(2,1)S(1)}, bf16[2,128,512]{2,1,0:T(8,128)(2,1)}, u32[]{:S(2)}) copy-start(bf16[2,128,512]{2,1,0:T(8,128)(2,1)} %param.17) | copy-start | bytes 786436
  7.2 77.8 %all-gather.6.cloned.1.call-start = ((), (), s32[]{:S(2)}) async-start(), calls=%async_computation.4 | async-start | bytes 2228224 | tf_op jit(solution)/shard_map/all_gather | solution.py:111
  38.1 11.5 %all-to-all-start.2 = ((f32[1,32,4,8]{3,2,0,1:T(4,128)}), f32[1,32,4,8]{3,2,0,1:T(4,128)S(1)}, u32[]{:S(2)}, u32[]{:S(2)}) async-start(f32[1,32,4,8]{3,2,0,1:T(4,128)} %copy.104), calls=%async_computation.2 | async-start | bytes 131072 | tf_op jit(solution)/shard_map/all_to_all | solution.py:143
  41.6 60.4 %all-gather.4.cloned.1.call-start = ((), (), s32[]{:S(2)}) async-start(), calls=%async_computation.3 | async-start | bytes 2228224 | tf_op jit(solution)/shard_map/all_gather | solution.py:123
  49.5 11.6 %all-to-all-start.1 = ((f32[1,32,4,8]{3,2,0,1:T(4,128)}), f32[1,32,4,8]{3,2,0,1:T(4,128)S(1)}, u32[]{:S(2)}, u32[]{:S(2)}) async-start(f32[1,32,4,8]{3,2,0,1:T(4,128)} %copy.95), calls=%async_computation.1 | async-start | bytes 131072 | tf_op jit(solution)/shard_map/all_to_all | solution.py:142
  61.1 21.3 %all-to-all-start = ((f32[1,32,4,8,128]{4,3,2,0,1:T(8,128)}), f32[1,32,4,8,128]{4,3,2,0,1:T(8,128)S(1)}, u32[]{:S(2)}, u32[]{:S(2)}) async-start(f32[1,32,4,8,128]{4,3,2,0,1:T(8,128)} %copy.94), calls=%async_computation | async-start | bytes 1048576 | tf_op jit(solution)/shard_map/all_to_all | solution.py:141
  89.6 5.7 %copy-start.1 = (f32[4,2048,64,8]{1,2,3,0:T(8,128)}, f32[4,2048,64,8]{1,2,3,0:T(8,128)S(1)}, u32[]{:S(2)}) copy-start(f32[4,2048,64,8]{1,2,3,0:T(8,128)S(1)} %get-tuple-element.9) | copy-start | bytes 50331652
Sparse Core Ops, SparseCore 0:
  10.1 44.8 all-gather.5
  57.2 44.6 all-gather.3
where the time goes:
time: 119 us
  waiting for transfers between devices  24.4 us (21%)
  blocking collectives  24.1 us (20%)
  matrix products  17.7 us (15%)
  local copies, waits for them, and re-layouts  15.9 us (13%)
  between operations  15.6 us (13%)
  starting transfers between devices  11.8 us (10%)
  other arithmetic  8.98 us (8%)
    all_gather x1, blocking collectives, body(): every_query = lax.all_gather(cont_queries, 'ctx', axis=0, tiled=True)  24.1 us
    all_to_all x1, waiting for transfers between devices, body(): lax.all_to_all(local_numer[None], 'ctx', split_axis=1, concat_axis=0, til...  16.9 us
    unnamed x11, local copies, waits for them, and re-layouts  12.3 us
    dot_general x2, matrix products, attend_piece(): jnp.einsum('rkgl,lkd->rkgd', probs.astype(jnp.bfloat16), value_heads, pre...  9.58 us
    dot_general x2, matrix products, attend_piece(): jnp.einsum('rkgd,lkd->rkgl', queries, key_heads, preferred_element_type=j...  5.89 us
    reduce_sum x2, other arithmetic, attend_piece(): row_sum = jnp.sum(probs, axis=-1)  5.49 us
    all_to_all x1, starting transfers between devices, body(): lax.all_to_all(local_max[None], 'ctx', split_axis=1, concat_axis=0, tiled...  4.68 us
    all_to_all x1, waiting for transfers between devices, body(): lax.all_to_all(local_max[None], 'ctx', split_axis=1, concat_axis=0, tiled...  4.64 us
  transfers between devices with their start and end apart: 5, of which 4 were waited for; matrix products, arithmetic and copies ran while one was open for 21% of the time, Pallas kernels for 0%

commit v1 on v0

--- a/solution.py
+++ b/solution.py
@@ -139,7 +139,12 @@
     )
     exchanged = (
         lax.all_to_all(local_numer[None], "ctx", split_axis=1, concat_axis=0, tiled=True),
-        lax.all_to_all(local_max[None], "ctx", split_axis=1, concat_axis=0, tiled=True),
+        jnp.concatenate(
+            lax.all_to_all(
+                jnp.stack(jnp.split(local_max[None], lax.axis_size("ctx"), axis=1)), "ctx", 0, 0
+            ),
+            axis=0,
+        ),
         lax.all_to_all(local_sum[None], "ctx", split_axis=1, concat_axis=0, tiled=True),
     )
     stacked = (exchanged[1], exchanged[2], exchanged[0])

time: 119 us -> 129 us (1.084)
  local copies, waits for them, and re-layouts: 15.9 us -> 26.3 us
  waiting for transfers between devices: 24.4 us -> 22.6 us
  starting transfers between devices: 11.8 us -> 13.1 us
    unnamed x11 -> x26, local copies, waits for them, and re-layouts: 12.3 us -> 21.3 us
    all_to_all x1, waiting for transfers between devices: 4.64 us -> 0.01 us  [body(): lax.all_to_all(jnp.stack(jnp.split(local_max[None], lax.axis_size('ctx'),...]
    all_to_all x1, waiting for transfers between devices: 1.29 us -> 4.85 us  [body(): lax.all_to_all(local_sum[None], 'ctx', split_axis=1, concat_axis=0, tiled...]
    all_to_all x1, starting transfers between devices: 3.5 us -> 5.97 us  [body(): lax.all_to_all(local_sum[None], 'ctx', split_axis=1, concat_axis=0, tiled...]
    split x0 -> x17, local copies, waits for them, and re-layouts: none -> 1.68 us  [body(): jnp.split(local_max[None], lax.axis_size('ctx'), axis=1)]
    all_gather x1, waiting for transfers between devices: 1.55 us -> 0.01 us  [body(): lax.all_gather(local_values, 'ctx', axis=0, tiled=True)]
  transfers between devices with their start and end apart: 5 -> 5, of which waited for: 4 -> 2; matrix products, arithmetic and copies ran while one was open for 21% -> 27% of each run, Pallas kernels for 0% -> 0%
where the time goes in v1:
time: 129 us; the launch traced here: 128 us
  local copies, waits for them, and re-layouts  26.3 us (20%)
  blocking collectives  24.1 us (19%)
  waiting for transfers between devices  22.6 us (18%)
  matrix products  17.5 us (14%)
  between operations  15.5 us (12%)
  starting transfers between devices  13.1 us (10%)
  other arithmetic  8.98 us (7%)
    all_gather x1, blocking collectives, body(): every_query = lax.all_gather(cont_queries, 'ctx', axis=0, tiled=True)  24.1 us
    unnamed x26, local copies, waits for them, and re-layouts  21.3 us
    all_to_all x1, waiting for transfers between devices, body(): lax.all_to_all(local_numer[None], 'ctx', split_axis=1, concat_axis=0, til...  17.7 us
    dot_general x2, matrix products, attend_piece(): jnp.einsum('rkgl,lkd->rkgd', probs.astype(jnp.bfloat16), value_heads, pre...  9.59 us
    all_to_all x1, starting transfers between devices, body(): lax.all_to_all(local_sum[None], 'ctx', split_axis=1, concat_axis=0, tiled...  5.97 us
    dot_general x2, matrix products, attend_piece(): jnp.einsum('rkgd,lkd->rkgl', queries, key_heads, preferred_element_type=j...  5.7 us
    reduce_sum x2, other arithmetic, attend_piece(): row_sum = jnp.sum(probs, axis=-1)  5.48 us
    all_to_all x1, waiting for transfers between devices, body(): lax.all_to_all(local_sum[None], 'ctx', split_axis=1, concat_axis=0, tiled...  4.85 us
  transfers between devices with their start and end apart: 5, of which 2 were waited for; matrix products, arithmetic and copies ran while one was open for 27% of the time, Pallas kernels for 0%

profile of v1, /device:TPU:0, one launch (start us, length us, event | category | flops | bytes accessed | tf_op | source)
XLA Modules:
  0.0 128.2 jit_solution(10867136808076851067)
XLA Ops:
  7.2 1.0 copy.35
  8.2 1.0 copy.36
  9.2 0.8 pad_maximum_fusion.1
  11.3 24.1 %all-gather = bf16[16,2,4096]{2,1,0:T(2,128)(2,1)S(1)} all-gather(bf16[1,2,4096]{2,1,0:T(2,128)(2,1)} %bitcast.151), channel_id=1, replica_groups=mesh['grp'=2,'ctx'=16] {'ctx'}, dimensions={0}, use_global_device_ids=true | all-gather | bytes 278528 | tf_op jit(solution)/shard_map/all_gather | solution.py:125
  35.4 0.2 reshape.243
  35.7 1.3 fusion.59
  38.6 0.6 constant_dynamic-update-slice_fusion.15
  39.3 0.6 constant_dynamic-update-slice_fusion.14
  39.9 0.6 constant_dynamic-update-slice_fusion.13
  40.4 0.6 constant_dynamic-update-slice_fusion.12
  41.0 0.6 constant_dynamic-update-slice_fusion.11
  41.6 0.6 constant_dynamic-update-slice_fusion.10
  42.2 0.6 constant_dynamic-update-slice_fusion.9
  42.8 0.6 constant_dynamic-update-slice_fusion.8
  43.4 0.6 constant_dynamic-update-slice_fusion.7
  44.0 0.6 constant_dynamic-update-slice_fusion.6
  44.6 0.6 constant_dynamic-update-slice_fusion.5
  45.2 0.6 constant_dynamic-update-slice_fusion.4
  45.8 0.6 constant_dynamic-update-slice_fusion.3
  46.4 0.6 constant_dynamic-update-slice_fusion.2
  47.0 0.6 constant_dynamic-update-slice_fusion.1
  47.6 0.6 constant_dynamic-update-slice_fusion
  48.2 3.5 %all-to-all-start.1 = ((f32[16,1,2,4,8]{4,3,2,1,0:T(4,128)}), f32[16,1,2,4,8]{4,3,2,1,0:T(4,128)S(1)}, u32[]{:S(2)}, u32[]{:S(2)}) async-start(f32[16,1,2,4,8]{4,3,2,1,0:T(4,128)} %constant_dynamic-update-slice_fusion), calls=%async_computation.1 | async-start | bytes 131072 | tf_op jit(solution)/shard_map/all_to_all | solution.py:143
  51.7 1.0 copy.33
  52.7 1.0 copy.34
  53.7 0.8 pad_maximum_fusion
  54.4 0.7 iota_compare_fusion
  55.2 0.4 fusion.21
  55.6 1.2 convolution_bitcast_fusion
  56.8 1.0 fusion.60
  57.8 0.2 fusion.33
  58.0 0.7 copy.66
  58.7 6.0 %all-to-all-start.2 = ((f32[1,32,4,8]{3,2,0,1:T(4,128)}), f32[1,32,4,8]{3,2,0,1:T(4,128)S(1)}, u32[]{:S(2)}, u32[]{:S(2)}) async-start(f32[1,32,4,8]{3,2,0,1:T(4,128)} %copy.66), calls=%async_computation.2 | async-start | bytes 131072 | tf_op jit(solution)/shard_map/all_to_all | solution.py:148
  64.7 1.1 copy.44
  65.8 1.1 copy.81
  67.0 4.9 %all-to-all-done.2 = f32[1,32,4,8]{3,2,0,1:T(4,128)S(1)} async-done(((f32[1,32,4,8]{3,2,0,1:T(4,128)}), f32[1,32,4,8]{3,2,0,1:T(4,128)S(1)}, u32[]{:S(2)}, u32[]{:S(2)}) %all-to-all-start.2) | async-done | bytes 4128 | tf_op jit(solution)/shard_map/all_to_all | solution.py:148
  71.8 3.6 %all-to-all-start = ((f32[1,32,4,8,128]{4,3,2,0,1:T(8,128)}), f32[1,32,4,8,128]{4,3,2,0,1:T(8,128)S(1)}, u32[]{:S(2)}, u32[]{:S(2)}) async-start(f32[1,32,4,8,128]{4,3,2,0,1:T(8,128)} %copy.44), calls=%async_computation | async-start | bytes 1048576 | tf_op jit(solution)/shard_map/all_to_all | solution.py:141
  75.7 0.5 copy.62
  76.2 17.7 %all-to-all-done = f32[1,32,4,8,128]{4,3,2,0,1:T(8,128)S(1)} async-done(((f32[1,32,4,8,128]{4,3,2,0,1:T(8,128)}), f32[1,32,4,8,128]{4,3,2,0,1:T(8,128)S(1)}, u32[]{:S(2)}, u32[]{:S(2)}) %all-to-all-start) | async-done | bytes 524320 | tf_op jit(solution)/shard_map/all_to_all | solution.py:141
  93.9 0.7 fusion.18
  94.6 1.2 fusion.15
  95.8 0.6 copy.116
  96.4 4.4 %fusion = (f32[64,4,8]{0,2,1:T(8,128)S(1)}, f32[4,2048,64,8]{1,2,3,0:T(8,128)S(1)}) fusion(pred[64,2048]{1,0:T(8,128)(4,1)S(1)} %and_or_fusion, bf16[2048,4,128,1]{0,2,3,1:T(8,128)(2,1)} %bitcast.144, bf16[64,4,8,128]{3,2,1,0:T(8,128)(2,1)S(1)} %bitcast.141), kind=kOutput, calls=%fused_computation.2 | convolution fusion | flops 1086322688 | bytes 19537920 | tf_op jit(solution)/shard_map/rkgd,lkd->rkgl/dot_general | solution.py:36
  100.9 5.7 %copy-done.1 = f32[4,2048,64,8]{1,2,3,0:T(8,128)} copy-done((f32[4,2048,64,8]{1,2,3,0:T(8,128)}, f32[4,2048,64,8]{1,2,3,0:T(8,128)S(1)}, u32[]{:S(2)}) %copy-start.1) | copy-done | bytes 16777240
  106.6 5.1 %fusion.1 = f32[64,4,8]{0,2,1:T(8,128)S(1)} fusion(f32[4,2048,64,8]{1,2,3,0:T(8,128)S(1)} %get-tuple-element.25, f32[64,4,8]{0,2,1:T(8,128)S(1)} %broadcast_maximum_fusion.1, pred[64,2048]{1,0:T(8,128)(4,1)S(1)} %and_or_fusion), kind=kLoop, calls=%fused_computation.3 | loop fusion | flops 20969472 | bytes 16924672 | tf_op jit(solution)/shard_map/reduce_sum | solution.py:43
  111.7 8.4 %divide_convert_fusion = bf16[64,4,8,128]{3,0,2,1:T(8,128)(2,1)S(1)} fusion(bf16[2048,4,128,1]{0,2,3,1:T(8,128)(2,1)} %bitcast.160, f32[4,2048,64,8]{1,2,3,0:T(8,128)} %copy-done.1, f32[64,4,8]{0,2,1:T(8,128)S(1)} %broadcast_maximum_fusion.1, pred[64,2048]{1,0:T(8,128)(4,1)S(1)} %and_or_fusion, f32[64,4,8]{0,2,1:T(8,128)S(1)} %fusion.1), kind=kOutput, calls=%fused_computation.19 | convolution fusion | flops 1095237632 | bytes 19546112 | tf_op jit(solution)/shard_map/rkgl,lkd->rkgd/dot_general | solution.py:44
  120.0 0.3 copy.40
  120.4 1.0 copy.115
  (38 shorter events, 2.1 us)
Async XLA Ops:
  7.2 49.6 %copy-start = (bf16[2,128,512]{2,1,0:T(8,128)(2,1)S(1)}, bf16[2,128,512]{2,1,0:T(8,128)(2,1)}, u32[]{:S(2)}) copy-start(bf16[2,128,512]{2,1,0:T(8,128)(2,1)} %param.17) | copy-start | bytes 786436
  7.2 89.2 %all-gather.6.cloned.1.call-start = ((), (), s32[]{:S(2)}) async-start(), calls=%async_computation.4 | async-start | bytes 2228224 | tf_op jit(solution)/shard_map/all_gather | solution.py:111
  48.2 10.6 %all-to-all-start.1 = ((f32[16,1,2,4,8]{4,3,2,1,0:T(4,128)}), f32[16,1,2,4,8]{4,3,2,1,0:T(4,128)S(1)}, u32[]{:S(2)}, u32[]{:S(2)}) async-start(f32[16,1,2,4,8]{4,3,2,1,0:T(4,128)} %constant_dynamic-update-slice_fusion), calls=%async_computation.1 | async-start | bytes 131072 | tf_op jit(solution)/shard_map/all_to_all | solution.py:143
  51.7 60.0 %all-gather.4.cloned.1.call-start = ((), (), s32[]{:S(2)}) async-start(), calls=%async_computation.3 | async-start | bytes 2228224 | tf_op jit(solution)/shard_map/all_gather | solution.py:123
  58.7 13.1 %all-to-all-start.2 = ((f32[1,32,4,8]{3,2,0,1:T(4,128)}), f32[1,32,4,8]{3,2,0,1:T(4,128)S(1)}, u32[]{:S(2)}, u32[]{:S(2)}) async-start(f32[1,32,4,8]{3,2,0,1:T(4,128)} %copy.66), calls=%async_computation.2 | async-start | bytes 131072 | tf_op jit(solution)/shard_map/all_to_all | solution.py:148
  71.8 22.0 %all-to-all-start = ((f32[1,32,4,8,128]{4,3,2,0,1:T(8,128)}), f32[1,32,4,8,128]{4,3,2,0,1:T(8,128)S(1)}, u32[]{:S(2)}, u32[]{:S(2)}) async-start(f32[1,32,4,8,128]{4,3,2,0,1:T(8,128)} %copy.44), calls=%async_computation | async-start | bytes 1048576 | tf_op jit(solution)/shard_map/all_to_all | solution.py:141
  100.8 5.7 %copy-start.1 = (f32[4,2048,64,8]{1,2,3,0:T(8,128)}, f32[4,2048,64,8]{1,2,3,0:T(8,128)S(1)}, u32[]{:S(2)}) copy-start(f32[4,2048,64,8]{1,2,3,0:T(8,128)S(1)} %get-tuple-element.25) | copy-start | bytes 50331652
Sparse Core Ops, SparseCore 0:
  10.1 44.1 all-gather.5
  56.5 45.3 all-gather.3
